TPU v7x, 32 devices: a whole 2x2x4 slice. The times are simulated.
32 devices in a mesh: row: 8 (over z, core), col: 4 (over y, x).
Axes of the slice: x: 2, y: 2, z: 4, core: 2. Of those that a mesh axis runs over, the one named last changes fastest.
Arguments:
- sire_index: int32 [1024], P('row'), may hold values from 0 to 4095
- dam_index: int32 [1024], P('row'), may hold values from -1 to 4095, as said below
- relatives: float32 [4096, 4, 2048], P('row', None, 'col'), may hold values from 0 to 1
- factor_blocks: float32 [6, 2048, 2048], P(None, 'row', 'col'), may hold values from -0.125 to 0.125
- inverses: float32 [4, 2048, 2048], P(None, 'col'), as said below
Outputs:
- relationship: float32 [4, 2048, 1024], P(None, 'col', 'row')
- border: float32 [4, 2048, 1024], P(None, 'col', 'row')
Inputs may be any that keep to these rules, and one draw needn't show every extreme that they name: `dam_index`: -1 marks an unknown dam; every other value is a row of relatives. `inverses`: lower triangular, with diagonal entries of 0.6 to 1.4.
All inputs are finite; a program needn't handle non-finite values.
Results may differ from a plain program's by a relative error of at most 0.0001.
Values sent between devices are 32-bit elements; how exact they have to be, the bound alone decides.
A program may use at most 128 MiB of HBM per device.

v0:
```python
import jax
import jax.numpy as jnp
from jax import lax
from jax.sharding import PartitionSpec as P


def product(left, right):
    return jnp.dot(left, right, precision=lax.Precision.HIGHEST, preferred_element_type=jnp.float32)


def fetch_rows(stacked):
    return lax.all_gather(stacked, "row", axis=0, tiled=True)


def per_device(sire_index, dam_index, relatives, factor_blocks, inverses):
    calf_dev = sire_index.shape[0]
    old_dev, blocks, block_cols = relatives.shape
    flat_rows = relatives.reshape(old_dev, blocks * block_cols)
    all_sires, all_dams = (
        lax.all_gather(sire_index, "row", axis=0, tiled=True),
        lax.all_gather(dam_index, "row", axis=0, tiled=True),
    )
    owned = lax.axis_index("row") * old_dev + lax.iota(jnp.int32, old_dev)
    picks = 0.5 * (
        (all_sires[:, None] == owned[None, :]).astype(jnp.float32)
        + (all_dams[:, None] == owned[None, :]).astype(jnp.float32)
    )
    mine = lax.psum_scatter(product(picks, flat_rows), "row", scatter_dimension=0, tiled=True)
    relation = mine.T
    relationship = relation.reshape(blocks, block_cols, calf_dev)
    solved = []
    for target in range(blocks):
        remain = relationship[target]
        if target > 0:
            needed = jnp.stack(
                [factor_blocks[target * (target - 1) // 2 + source] for source in range(target)],
                axis=1,
            )
            whole_rows = fetch_rows(needed).reshape(-1, target * block_cols)
            earlier = jnp.concatenate(solved, axis=0)

            def earlier_terms(start, count, whole_rows=whole_rows, earlier=earlier):
                return product(whole_rows, earlier)

            remain = remain - lax.psum_scatter(
                earlier_terms(jnp.int32(0), block_cols * lax.axis_size("col")),
                "col",
                scatter_dimension=0,
                tiled=True,
            )
        own_inverse = inverses[target]
        solved.append(product(own_inverse, lax.all_gather(remain, "col", axis=0, tiled=True)))
    return (relationship, jnp.stack(solved))


def solution(mesh):
    return jax.shard_map(
        per_device,
        mesh=mesh,
        in_specs=(
            P("row"),
            P("row"),
            P("row", None, "col"),
            P(None, "row", "col"),
            P(None, "col", None),
        ),
        out_specs=(P(None, "col", "row"), P(None, "col", "row")),
        check_vma=False,
    )
```

profile of v0, /device:TPU:0, one launch (start us, length us, event | category | flops | bytes accessed | tf_op | source)
XLA Modules:
  0.0 627.8 jit_solution(4835952748387480247)
XLA Ops:
  7.2 0.0 reduce-scatter.5.cloned.1.call-start
  7.2 6.1 copy.33
  13.4 13.4 %all-gather.1 = s32[8,1,128]{2,1,0:T(1,128)S(1)} all-gather(s32[1,1,128]{2,1,0:T(1,128)S(1)} %bitcast.82), channel_id=1, replica_groups=mesh['row'=8,'col'=4] {'row'}, dimensions={0}, use_global_device_ids=true | all-gather | bytes 4608 | tf_op jit(solution)/shard_map/all_gather | solution.py:20
  26.8 8.7 %all-gather.2 = s32[8,1,128]{2,1,0:T(1,128)S(1)} all-gather(s32[1,1,128]{2,1,0:T(1,128)S(1)} %bitcast.83), channel_id=1, replica_groups=mesh['row'=8,'col'=4] {'row'}, dimensions={0}, use_global_device_ids=true | all-gather | bytes 4608 | tf_op jit(solution)/shard_map/all_gather | solution.py:21
  35.5 17.8 %fusion.17 = f32[1024,2048]{1,0:T(8,128)} fusion(f32[512,2048]{1,0:T(8,128)} %bitcast.68, s32[512]{0:T(512)S(1)} %iota_add_fusion, s32[1024]{0:T(1024)S(1)} %bitcast.81, s32[1024]{0:T(1024)S(1)} %bitcast.80), kind=kOutput, calls=%fused_computation.15 | convolution fusion | flops 12888047616 | bytes 12593152 | tf_op jit(solution)/shard_map/dot_general | solution.py:8
  53.4 0.0 all-gather.11.cloned.1.call-start
  53.5 89.0 %reduce-scatter.5.cloned.1.call-done = f32[128,2048]{1,0:T(8,128)} async-done(((f32[1024,2048]{1,0:T(8,128)}), f32[128,2048]{1,0:T(8,128)}) %reduce-scatter.5.cloned.1.call-update) | async-done | bytes 1048592 | tf_op jit(solution)/shard_map/reduce_scatter | solution.py:28
  142.4 1.7 slice.60
  144.1 0.0 all-gather.23.cloned.1.call-start
  144.2 3.2 fusion.44
  147.4 0.2 reduce-scatter.7.cloned.1.call-start
  147.6 21.7 %all-gather.11.cloned.1.call-done = f32[2048,128]{0,1:T(8,128)} async-done(((f32[512,128]{0,1:T(8,128)}), f32[2048,128]{0,1:T(8,128)}) %all-gather.11.cloned.1.call-update) | async-done | bytes 1048592 | tf_op jit(solution)/shard_map/all_gather | solution.py:52
  169.3 6.9 %fusion.8 = f32[128,512]{1,0:T(8,128)S(1)} fusion(f32[2048,128]{0,1:T(8,128)} %all-gather.11.cloned.1.call-done, f32[4,512,2048]{2,1,0:T(8,128)} %param.9), kind=kOutput, calls=%fused_computation.8 | convolution fusion | flops 1610612736 | bytes 5505024 | tf_op jit(solution)/shard_map/dot_general | solution.py:8
  176.1 42.2 %all-gather.23.cloned.1.call-done = f32[1,2048,512]{2,1,0:T(8,128)} async-done(((f32[1,256,512]{2,1,0:T(8,128)}), f32[1,2048,512]{2,1,0:T(8,128)}) %all-gather.23.cloned.1.call-update) | async-done | bytes 4194320 | tf_op jit(solution)/shard_map/all_gather | solution.py:12
  218.3 7.5 %fusion.14 = f32[2048,128]{0,1:T(8,128)} fusion(f32[128,512]{1,0:T(8,128)S(1)} %fusion.8, f32[1,2048,512]{2,1,0:T(8,128)} %all-gather.23.cloned.1.call-done), kind=kOutput, calls=%fused_computation.14 | convolution fusion | flops 1610612736 | bytes 5505024 | tf_op jit(solution)/shard_map/dot_general | solution.py:8
  225.8 0.0 all-gather.13.cloned.1.call-start
  225.9 26.8 %reduce-scatter.7.cloned.1.call-done = f32[512,128]{0,1:T(8,128)} async-done(((f32[2048,128]{0,1:T(8,128)}), f32[512,128]{0,1:T(8,128)}) %reduce-scatter.7.cloned.1.call-update) | async-done | bytes 262160 | tf_op jit(solution)/shard_map/reduce_scatter | solution.py:45
  252.7 1.7 slice_subtract_fusion.2
  254.4 0.0 all-gather.15.cloned.1.call-start
  254.5 2.1 copy.28
  256.5 2.0 copy.29
  258.6 2.2 pad_maximum_fusion.1
  260.8 0.3 reduce-scatter.9.cloned.1.call-start
  261.1 20.0 %all-gather.13.cloned.1.call-done = f32[2048,128]{0,1:T(8,128)} async-done(((f32[512,128]{0,1:T(8,128)}), f32[2048,128]{0,1:T(8,128)}) %all-gather.13.cloned.1.call-update) | async-done | bytes 1048592 | tf_op jit(solution)/shard_map/all_gather | solution.py:52
  281.1 6.9 %fusion.4 = f32[128,512]{1,0:T(8,128)S(1)} fusion(f32[2048,128]{0,1:T(8,128)} %all-gather.13.cloned.1.call-done, f32[4,512,2048]{2,1,0:T(8,128)} %param.9), kind=kOutput, calls=%fused_computation.4 | convolution fusion | flops 1610612736 | bytes 5505024 | tf_op jit(solution)/shard_map/dot_general | solution.py:8
  287.9 77.2 %all-gather.15.cloned.1.call-done = f32[2048,2,512]{0,2,1:T(8,128)} async-done(((f32[256,2,512]{0,2,1:T(8,128)}), f32[2048,2,512]{0,2,1:T(8,128)}) %all-gather.15.cloned.1.call-update) | async-done | bytes 8388624 | tf_op jit(solution)/shard_map/all_gather | solution.py:12
  365.2 8.1 %fusion.37 = f32[2048,128]{0,1:T(8,128)} fusion(f32[2048,1024]{0,1:T(8,128)} %bitcast.58, f32[512,128]{0,1:T(8,128)S(1)} %bitcast.69, f32[512,128]{0,1:T(8,128)S(1)} %bitcast.59), kind=kOutput, calls=%fused_computation.36 | convolution fusion | flops 3221356544 | bytes 9961472 | tf_op jit(solution)/shard_map/dot_general | solution.py:8
  373.3 0.0 all-gather.17.cloned.1.call-start
  373.3 26.5 %reduce-scatter.9.cloned.1.call-done = f32[512,128]{0,1:T(8,128)} async-done(((f32[2048,128]{0,1:T(8,128)}), f32[512,128]{0,1:T(8,128)}) %reduce-scatter.9.cloned.1.call-update) | async-done | bytes 262160 | tf_op jit(solution)/shard_map/reduce_scatter | solution.py:45
  399.8 1.7 slice_subtract_fusion.1
  401.6 0.0 all-gather.19.cloned.1.call-start
  401.6 1.0 copy.30
  402.6 0.2 copy.31
  402.8 0.2 copy.32
  403.0 2.3 pad_maximum_fusion
  405.4 0.3 reduce-scatter.11.cloned.1.call-start
  405.7 23.1 %all-gather.17.cloned.1.call-done = f32[2048,128]{0,1:T(8,128)} async-done(((f32[512,128]{0,1:T(8,128)}), f32[2048,128]{0,1:T(8,128)}) %all-gather.17.cloned.1.call-update) | async-done | bytes 1048592 | tf_op jit(solution)/shard_map/all_gather | solution.py:52
  428.8 6.9 %fusion.2 = f32[128,512]{1,0:T(8,128)S(1)} fusion(f32[2048,128]{0,1:T(8,128)} %all-gather.17.cloned.1.call-done, f32[4,512,2048]{2,1,0:T(8,128)} %param.9), kind=kOutput, calls=%fused_computation.2 | convolution fusion | flops 1610612736 | bytes 5505024 | tf_op jit(solution)/shard_map/dot_general | solution.py:8
  435.7 111.5 %all-gather.19.cloned.1.call-done = f32[2048,3,512]{0,2,1:T(8,128)} async-done(((f32[256,3,512]{0,2,1:T(8,128)}), f32[2048,3,512]{0,2,1:T(8,128)}) %all-gather.19.cloned.1.call-update) | async-done | bytes 12582928 | tf_op jit(solution)/shard_map/all_gather | solution.py:12
  547.2 10.6 %fusion.31 = f32[2048,128]{0,1:T(8,128)} fusion(f32[2048,1536]{0,1:T(8,128)} %bitcast.57, f32[512,128]{0,1:T(8,128)S(1)} %bitcast.72, f32[512,128]{0,1:T(8,128)S(1)} %bitcast.70, f32[512,128]{0,1:T(8,128)S(1)} %bitcast.60), kind=kOutput, calls=%fused_computation.30 | convolution fusion | flops 4832231424 | bytes 14417920 | tf_op jit(solution)/shard_map/dot_general | solution.py:8
  557.8 0.0 all-gather.21.cloned.1.call-start
  557.9 26.2 %reduce-scatter.11.cloned.1.call-done = f32[512,128]{0,1:T(8,128)} async-done(((f32[2048,128]{0,1:T(8,128)}), f32[512,128]{0,1:T(8,128)}) %reduce-scatter.11.cloned.1.call-update) | async-done | bytes 262160 | tf_op jit(solution)/shard_map/reduce_scatter | solution.py:45
  584.1 1.7 slice_subtract_fusion
  585.8 1.3 copy.27
  587.1 26.0 %all-gather.21.cloned.1.call-done = f32[2048,128]{0,1:T(8,128)} async-done(((f32[512,128]{0,1:T(8,128)}), f32[2048,128]{0,1:T(8,128)}) %all-gather.21.cloned.1.call-update) | async-done | bytes 1048592 | tf_op jit(solution)/shard_map/all_gather | solution.py:52
  613.0 6.9 %fusion.24 = f32[1,512,128]{1,2,0:T(8,128)S(1)} fusion(f32[2048,128]{0,1:T(8,128)} %all-gather.21.cloned.1.call-done, f32[4,512,2048]{2,1,0:T(8,128)} %param.9), kind=kOutput, calls=%fused_computation.23 | convolution fusion | flops 1610612736 | bytes 5505024 | tf_op jit(solution)/shard_map/dot_general | solution.py:8
  619.9 0.1 pad_maximum_fusion.2
  620.0 1.3 copy.24
  (18 shorter events, 0.2 us)
Async XLA Ops:
  7.2 135.3 %reduce-scatter.5.cloned.1.call-start = ((), (), s32[]{:S(2)}) async-start(), calls=%async_computation.4 | async-start | bytes 9437184 | tf_op jit(solution)/shard_map/reduce_scatter | solution.py:28
  7.2 6.2 copy-start.1
  7.2 19.6 %copy-start.2 = (s32[128]{0:T(128)S(1)}, s32[128]{0:T(128)}, u32[]{:S(2)}) copy-start(s32[128]{0:T(128)} %param.6) | copy-start | bytes 1540
  53.4 115.8 %all-gather.11.cloned.1.call-start = ((), (), s32[]{:S(2)}) async-start(), calls=%async_computation.5 | async-start | bytes 1310720 | tf_op jit(solution)/shard_map/all_gather | solution.py:52
  144.1 74.2 %all-gather.23.cloned.1.call-start = ((), (), s32[]{:S(2)}) async-start(), calls=%async_computation.14 | async-start | bytes 4718592 | tf_op jit(solution)/shard_map/all_gather | solution.py:12
  147.4 105.3 %reduce-scatter.7.cloned.1.call-start = ((), (), s32[]{:S(2)}) async-start(), calls=%async_computation.6 | async-start | bytes 1310720 | tf_op jit(solution)/shard_map/reduce_scatter | solution.py:45
  176.1 76.6 %copy-start = (f32[128,2048]{1,0:T(8,128)S(1)}, f32[128,2048]{1,0:T(8,128)}, u32[]{:S(2)}) copy-start(f32[128,2048]{1,0:T(8,128)} %reduce-scatter.5.cloned.1.call-done) | copy-start | bytes 3145732
  225.8 55.3 %all-gather.13.cloned.1.call-start = ((), (), s32[]{:S(2)}) async-start(), calls=%async_computation.7 | async-start | bytes 1310720 | tf_op jit(solution)/shard_map/all_gather | solution.py:52
  254.4 110.8 %all-gather.15.cloned.1.call-start = ((), (), s32[]{:S(2)}) async-start(), calls=%async_computation.8 | async-start | bytes 9437184 | tf_op jit(solution)/shard_map/all_gather | solution.py:12
  260.8 139.0 %reduce-scatter.9.cloned.1.call-start = ((), (), s32[]{:S(2)}) async-start(), calls=%async_computation.9 | async-start | bytes 1310720 | tf_op jit(solution)/shard_map/reduce_scatter | solution.py:45
  373.3 55.5 %all-gather.17.cloned.1.call-start = ((), (), s32[]{:S(2)}) async-start(), calls=%async_computation.10 | async-start | bytes 1310720 | tf_op jit(solution)/shard_map/all_gather | solution.py:52
  401.6 145.6 %all-gather.19.cloned.1.call-start = ((), (), s32[]{:S(2)}) async-start(), calls=%async_computation.11 | async-start | bytes 14155776 | tf_op jit(solution)/shard_map/all_gather | solution.py:12
  405.4 178.7 %reduce-scatter.11.cloned.1.call-start = ((), (), s32[]{:S(2)}) async-start(), calls=%async_computation.12 | async-start | bytes 1310720 | tf_op jit(solution)/shard_map/reduce_scatter | solution.py:45
  557.8 55.2 %all-gather.21.cloned.1.call-start = ((), (), s32[]{:S(2)}) async-start(), calls=%async_computation.13 | async-start | bytes 1310720 | tf_op jit(solution)/shard_map/all_gather | solution.py:52
Sparse Core Ops, SparseCore 0:
  53.5 88.8 reduce-scatter.4
  144.3 24.9 all-gather.10
  171.4 46.8 all-gather.22
  225.9 26.7 reduce-scatter.6
  254.5 26.4 all-gather.12
  283.1 82.0 all-gather.14
  373.4 26.4 reduce-scatter.8
  402.3 26.4 all-gather.16
  430.4 116.6 all-gather.18
  557.9 26.0 reduce-scatter.10
  586.5 26.4 all-gather.20
where the time goes:
time: 628 us
  waiting for transfers between devices  490 us (78%)
  matrix products  71.4 us (11%)
  blocking collectives  22.2 us (4%)
  local copies, waits for them, and re-layouts  19.1 us (3%)
  between operations  14 us (2%)
  other arithmetic  9.71 us (2%)
    all_gather x3, waiting for transfers between devices, fetch_rows(): return lax.all_gather(stacked, 'row', axis=0, tiled=True)  231 us
    all_gather x4, waiting for transfers between devices, per_device(): lax.all_gather(remain, 'col', axis=0, tiled=True)  90.7 us
    reduce_scatter x1, waiting for transfers between devices, per_device(): lax.psum_scatter(product(picks, flat_rows), 'row', scatter_dimension=0, t...  89 us
    reduce_scatter x3, waiting for transfers between devices, per_device(): lax.psum_scatter(earlier_terms(jnp.int32(0), block_cols * lax.axis_size('...  79.6 us
    dot_general x8, matrix products, product(): jnp.dot(left, right, precision=lax.Precision.HIGHEST, preferred_element_t...  71.4 us
    unnamed x14, local copies, waits for them, and re-layouts  14.2 us
    all_gather x1, blocking collectives, per_device(): lax.all_gather(sire_index, 'row', axis=0, tiled=True)  13.4 us
  transfers between devices with their start and end apart: 11, of which 11 were waited for; matrix products, arithmetic and copies ran while one was open for 6% of the time, Pallas kernels for 0%

commit v1 on v0

v1 whole, which is shorter than its diff:
```python
import functools
import jax
import jax.numpy as jnp
from jax import lax
from jax.experimental import pallas as pl
from jax.experimental.pallas import tpu as pltpu
from jax.sharding import PartitionSpec as P

MESH = pl.DeviceIdType.MESH


def split(value):
    high = value.astype(jnp.bfloat16)
    return high, (value - high.astype(jnp.float32)).astype(jnp.bfloat16)


def split_exact(value):
    high = lax.reduce_precision(value, 8, 7)
    low = lax.reduce_precision(value - high, 8, 7)
    return high.astype(jnp.bfloat16), low.astype(jnp.bfloat16)


def mxu(left, right):
    return jnp.dot(left, right, preferred_element_type=jnp.float32)


def wide_product(left_high, left_low, right):
    right_high, right_low = split(right)
    return mxu(left_high, right_high) + (mxu(left_high, right_low) + mxu(left_low, right_high))


def narrow_product(left, right):
    width = right.shape[1]
    left_high, left_low = split(left)
    right_high, right_low = split(right)
    both = mxu(left_high, jnp.concatenate([right_high, right_low], axis=1))
    return both[:, :width] + (both[:, width:] + mxu(left_low, right_high))


def gather_start(cols, r, c, own_ref, slots, send, recv):
    copies = []
    for step in range(1, cols):
        copies.append(
            pltpu.make_async_remote_copy(
                src_ref=own_ref, dst_ref=slots.at[c], send_sem=send.at[step], recv_sem=recv.at[c],
                device_id=(r, (c + step) % cols), device_id_type=MESH,
            )
        )
    for copy in copies:
        copy.start()
    slots[c] = own_ref[...]
    return copies


def gather_wait(cols, r, c, slots, send, recv):
    for step in range(1, cols):
        source = (c + step) % cols
        slot = slots.at[source]
        pltpu.make_async_remote_copy(
            src_ref=slot, dst_ref=slot, send_sem=send.at[step], recv_sem=recv.at[source],
            device_id=(r, source), device_id_type=MESH,
        ).wait_recv()


def first_kernel(target, cols, relation_ref, inverse_hbm, out_ref, related, inverse, inv_sem, rel_send, rel_recv):
    r, c = lax.axis_index("row"), lax.axis_index("col")
    load = pltpu.make_async_copy(inverse_hbm.at[target], inverse, inv_sem)
    load.start()
    barrier = pltpu.get_barrier_semaphore()
    for step in range(1, cols):
        pl.semaphore_signal(barrier, inc=1, device_id=(r, (c + step) % cols), device_id_type=MESH)
    pl.semaphore_wait(barrier, cols - 1)
    copies = gather_start(cols, r, c, relation_ref, related, rel_send, rel_recv)
    load.wait()
    gather_wait(cols, r, c, related, rel_send, rel_recv)
    out_ref[...] = narrow_product(inverse[...], related[...].reshape(-1, relation_ref.shape[1]))
    for copy in copies:
        copy.wait_send()


def first_step(cols, relation, inverses):
    dma = pltpu.SemaphoreType.DMA
    return pl.pallas_call(
        functools.partial(first_kernel, 0, cols),
        out_shape=jax.ShapeDtypeStruct(relation.shape, jnp.float32),
        in_specs=[pl.BlockSpec(memory_space=pltpu.VMEM), pl.BlockSpec(memory_space=pl.ANY)],
        out_specs=pl.BlockSpec(memory_space=pltpu.VMEM),
        scratch_shapes=[
            pltpu.VMEM((cols,) + relation.shape, jnp.float32),
            pltpu.VMEM(inverses.shape[1:], jnp.float32),
            dma, dma((cols,)), dma((cols,)),
        ],
        compiler_params=pltpu.CompilerParams(
            collective_id=0, has_side_effects=True, vmem_limit_bytes=40 * 1024 * 1024
        ),
        cost_estimate=pl.CostEstimate(flops=10**9, bytes_accessed=60 * 10**6, transcendentals=0),
        name="first_step",
    )(relation, inverses)


def step_kernel(target, rows, cols, later, has_sum, *refs):
    refs = list(refs)
    border_ref, relation_ref, inverse_hbm = refs[:3]
    refs = refs[3:]
    factor_refs, refs = refs[: 1 + later], refs[1 + later :]
    if has_sum:
        sum_refs, refs = refs[: 1 + later], refs[1 + later :]
    else:
        sum_refs = None
    out_ref, refs = refs[0], refs[1:]
    sum_outs, refs = refs[:later], refs[later:]
    (
        calves, partial, landed, reduced, whole, inverse, related,
        inv_sem, rel_send, rel_recv, chip_send, chip_recv, core_send, core_recv,
        red_send, red_recv, swap_send, swap_recv, wide_send, wide_recv,
    ) = refs
    r, c = lax.axis_index("row"), lax.axis_index("col")
    chips = rows // 2
    z, core = r // 2, r % 2
    partner = 2 * z + 1 - core
    width = border_ref.shape[1]
    short = reduced.shape[0]

    load = pltpu.make_async_copy(inverse_hbm.at[target], inverse, inv_sem)
    load.start()

    barrier = pltpu.get_barrier_semaphore()
    for step in range(1, rows):
        pl.semaphore_signal(barrier, inc=1, device_id=((r + step) % rows, c), device_id_type=MESH)
    for step in range(1, cols):
        pl.semaphore_signal(barrier, inc=1, device_id=(r, (c + step) % cols), device_id_type=MESH)
    pl.semaphore_wait(barrier, rows + cols - 2)

    def lanes(owner):
        return pl.ds(pl.multiple_of(owner * width, width), width)

    def remote(src, dst, send, recv, target):
        return pltpu.make_async_remote_copy(
            src_ref=src, dst_ref=dst, send_sem=send, recv_sem=recv, device_id=target, device_id_type=MESH
        )

    own = calves.at[:, lanes(r)]
    first = [remote(border_ref, own, chip_send.at[0], core_recv.at[z], (partner, c))]
    for step in range(1, chips):
        there = (z + step) % chips
        first.append(remote(border_ref, own, chip_send.at[step], chip_recv.at[z], (2 * there + core, c)))
    for copy in first:
        copy.start()
    fifth = gather_start(cols, r, c, relation_ref, related, rel_send, rel_recv)
    calves[:, lanes(r)] = border_ref[...]
    second = []
    for step in range(1, chips):
        source = (z + step) % chips
        slot = calves.at[:, lanes(2 * source + core)]
        remote(slot, slot, chip_send.at[step], chip_recv.at[source], (partner, c)).wait_recv()
        copy = remote(slot, slot, core_send.at[step], core_recv.at[source], (partner, c))
        copy.start()
        second.append(copy)
    for step in range(chips):
        source = (z + step) % chips
        slot = calves.at[:, lanes(2 * source + 1 - core)]
        remote(slot, slot, core_send.at[step], core_recv.at[source], (partner, c)).wait_recv()

    tile = 2 * width

    def multiply(factor_ref, sum_ref, result):
        high, low = split(factor_ref[...])

        def body(index, carry):
            span = pl.ds(pl.multiple_of(index * tile, tile), tile)
            value = wide_product(high, low, calves[:, span])
            if sum_ref is not None:
                value = value + sum_ref[:, span]
            result[:, span] = value
            return carry

        lax.fori_loop(0, calves.shape[1] // tile, body, 0)

    multiply(factor_refs[0], sum_refs[0] if has_sum else None, partial)

    def band(owner):
        return pl.ds(pl.multiple_of(owner * short, short), short)

    third = []
    for step in range(1, cols):
        there = (c + step) % cols
        copy = remote(partial.at[band(there), :], landed.at[c], red_send.at[step], red_recv.at[c], (r, there))
        copy.start()
        third.append(copy)
    for index in range(later):
        multiply(factor_refs[1 + index], sum_refs[1 + index] if has_sum else None, sum_outs[index])
    total = partial[band(c), :]
    for step in range(1, cols):
        source = (c + step) % cols
        slot = landed.at[source]
        remote(slot, slot, red_send.at[step], red_recv.at[source], (r, source)).wait_recv()
        total = total + landed[source]
    reduced[...] = total

    fourth = []
    for step in range(1, rows):
        there = (r + step) % rows
        copy = remote(reduced.at[:, lanes(there)], whole.at[r, c], swap_send.at[step], swap_recv.at[r], (there, c))
        copy.start()
        fourth.append(copy)
    whole[r, c] = reduced[:, lanes(r)]

    def spread(source, action):
        for step in range(1, cols):
            there = (c + step) % cols
            slot = whole.at[source, c]
            action(remote(slot, slot, wide_send.at[source, step], wide_recv.at[source, c], (r, there)))

    spread(r, lambda copy: copy.start())
    for step in range(1, rows):
        source = (r + step) % rows
        slot = whole.at[source, c]
        remote(slot, slot, swap_send.at[step], swap_recv.at[source], (source, c)).wait_recv()
        spread(source, lambda copy: copy.start())
    for source in range(rows):
        for step in range(1, cols):
            there = (c + step) % cols
            slot = whole.at[source, there]
            remote(slot, slot, wide_send.at[source, step], wide_recv.at[source, there], (r, there)).wait_recv()

    load.wait()
    gather_wait(cols, r, c, related, rel_send, rel_recv)
    remain = (related[...] - whole[...].reshape(related.shape)).reshape(-1, width)
    out_ref[...] = narrow_product(inverse[...], remain)

    for copy in first + second + third + fourth + fifth:
        copy.wait_send()
    for source in range(rows):
        spread(source, lambda copy: copy.wait_send())


def block_step(rows, cols, target, border, relation, inverses, factors, sums):
    later = len(factors) - 1
    band, depth = factors[0].shape
    width = border.shape[1]
    short = band // cols
    dma = pltpu.SemaphoreType.DMA
    f32 = jnp.float32
    vmem = pl.BlockSpec(memory_space=pltpu.VMEM)
    out = pl.pallas_call(
        functools.partial(step_kernel, target, rows, cols, later, bool(sums)),
        out_shape=[jax.ShapeDtypeStruct(border.shape, f32)]
        + [jax.ShapeDtypeStruct((band, rows * width), f32)] * later,
        in_specs=[vmem, vmem, pl.BlockSpec(memory_space=pl.ANY)] + [vmem] * (len(factors) + len(sums)),
        out_specs=[vmem] * (1 + later),
        scratch_shapes=[
            pltpu.VMEM((depth, rows * width), f32),
            pltpu.VMEM((band, rows * width), f32),
            pltpu.VMEM((cols, short, rows * width), f32),
            pltpu.VMEM((short, rows * width), f32),
            pltpu.VMEM((rows, cols, short, width), f32),
            pltpu.VMEM(inverses.shape[1:], f32),
            pltpu.VMEM((cols,) + relation.shape, f32),
            dma, dma((cols,)), dma((cols,)),
            dma((rows // 2,)), dma((rows // 2,)), dma((rows // 2,)), dma((rows // 2,)),
            dma((cols,)), dma((cols,)), dma((rows,)), dma((rows,)), dma((rows, cols)), dma((rows, cols)),
        ],
        compiler_params=pltpu.CompilerParams(
            collective_id=target, has_side_effects=True, vmem_limit_bytes=40 * 1024 * 1024
        ),
        cost_estimate=pl.CostEstimate(flops=10**9, bytes_accessed=200 * 10**6, transcendentals=0),
        name="block_step_%d" % target,
    )(border, relation, inverses, *factors, *sums)
    return out[0], list(out[1:])


def per_device(rows, cols, sire_index, dam_index, relatives, factor_blocks, inverses):
    calf_dev = sire_index.shape[0]
    old_dev, blocks, block_cols = relatives.shape
    both = lax.all_gather(jnp.stack([sire_index, dam_index]), "row", axis=1, tiled=True)
    owned = lax.axis_index("row") * old_dev + lax.iota(jnp.int32, old_dev)
    picks = 0.5 * (
        (both[0][:, None] == owned[None, :]).astype(jnp.float32)
        + (both[1][:, None] == owned[None, :]).astype(jnp.float32)
    )
    picks = picks.astype(jnp.bfloat16)
    relationship = []
    for target in range(blocks):
        high, low = split_exact(relatives[:, target, :])
        shares = mxu(picks, high) + mxu(picks, low)
        relationship.append(lax.psum_scatter(shares, "row", scatter_dimension=0, tiled=True).T)
    solved = [first_step(cols, relationship[0], inverses)]
    sums = []
    for target in range(1, blocks):
        source = target - 1
        factors = [factor_blocks[t * (t - 1) // 2 + source] for t in range(target, blocks)]
        border, sums = block_step(
            rows, cols, target, solved[-1], relationship[target], inverses, factors, sums
        )
        solved.append(border)
    relationship, last = lax.optimization_barrier((relationship, solved[-1]))
    return (jnp.stack(relationship), jnp.stack(solved[:-1] + [last]))


def solution(mesh):
    return jax.shard_map(
        functools.partial(per_device, mesh.shape["row"], mesh.shape["col"]),
        mesh=mesh,
        in_specs=(
            P("row"),
            P("row"),
            P("row", None, "col"),
            P(None, "row", "col"),
            P(None, "col", None),
        ),
        out_specs=(P(None, "col", "row"), P(None, "col", "row")),
        check_vma=False,
    )
```

time: 628 us -> 323 us (0.51)
  waiting for transfers between devices: 490 us -> 43.6 us
  Pallas kernels: 0 us -> 212 us
  matrix products: 71.4 us -> 14.3 us
  blocking collectives: 22.2 us -> 13.5 us
  other arithmetic: 9.71 us -> 2.15 us
    all_gather x7 -> x0, waiting for transfers between devices: 322 us -> none  [the longest x3 231 us: fetch_rows(): return lax.all_gather(stacked, 'row', axis=0, tiled=True)]
    pallas_call x0 -> x4, Pallas kernels: none -> 212 us  [the longest x3 199 us: block_step(): pl.pallas_call(functools.partial(step_kernel, target, rows, cols, later,...]
    reduce_scatter x4, waiting for transfers between devices: 169 us -> 43.5 us  [per_device(): lax.psum_scatter(shares, 'row', scatter_dimension=0, tiled=True)]
    dot_general x8, matrix products: 71.4 us -> 14.3 us  [mxu(): return jnp.dot(left, right, preferred_element_type=jnp.float32)]
    all_gather x2 -> x1, blocking collectives: 22.2 us -> 13.5 us  [per_device(): lax.all_gather(jnp.stack([sire_index, dam_index]), 'row', axis=1, tiled=T...]
    unnamed x14 -> x28, local copies, waits for them, and re-layouts: 14.2 us -> 9.86 us
  transfers between devices with their start and end apart: 11 -> 4, of which waited for: 11 -> 2; matrix products, arithmetic and copies ran while one was open for 6% -> 4% of each run, Pallas kernels for 0% -> 46%
where the time goes in v1:
time: 323 us; the launch traced here: 322 us
  Pallas kernels  212 us (66%)
  waiting for transfers between devices  43.6 us (13%)
  local copies, waits for them, and re-layouts  22.4 us (7%)
  matrix products  14.3 us (4%)
  between operations  13.9 us (4%)
  blocking collectives  13.5 us (4%)
    pallas_call x3, Pallas kernels, block_step(): pl.pallas_call(functools.partial(step_kernel, target, rows, cols, later,...  199 us
    reduce_scatter x4, waiting for transfers between devices, per_device(): lax.psum_scatter(shares, 'row', scatter_dimension=0, tiled=True)  43.5 us
    dot_general x8, matrix products, mxu(): return jnp.dot(left, right, preferred_element_type=jnp.float32)  14.3 us
    all_gather x1, blocking collectives, per_device(): lax.all_gather(jnp.stack([sire_index, dam_index]), 'row', axis=1, tiled=T...  13.5 us
    pallas_call x1, Pallas kernels, first_step(): pl.pallas_call(functools.partial(first_kernel, 0, cols), out_shape=jax.Sh...  13.3 us
    slice x1, local copies, waits for them, and re-layouts, per_device(): high, low = split_exact(relatives[:, target, :])  10.4 us
    unnamed x28, local copies, waits for them, and re-layouts  9.86 us
  transfers between devices with their start and end apart: 4, of which 2 were waited for; matrix products, arithmetic and copies ran while one was open for 4% of the time, Pallas kernels for 46%

profile of v1, /device:TPU:0, one launch (start us, length us, event | category | flops | bytes accessed | tf_op | source)
XLA Modules:
  0.0 322.3 jit_solution(16129902893762767067)
XLA Ops:
  7.2 0.0 reduce-scatter.5.cloned.1.call-start
  7.2 0.7 pad_add_fusion
  7.9 13.5 %all_gather.3 = s32[2,1024]{1,0:T(2,128)S(1)} all-gather(s32[2,128]{1,0:T(2,128)S(1)} %pad_add_fusion), channel_id=1, replica_groups=mesh['row'=8,'col'=4] {'row'}, dimensions={1}, use_global_device_ids=true | all-gather | bytes 9216 | tf_op jit(solution)/shard_map/all_gather | solution.py:275
  21.4 10.4 %fusion.56 = (f32[512,1,512]{2,1,0:T(1,128)S(1)}, f32[512,1,512]{2,1,0:T(1,128)S(1)}, f32[512,1,512]{2,1,0:T(1,128)S(1)}, f32[512,1,512]{2,1,0:T(1,128)S(1)}) fusion(f32[512,4,512]{2,1,0:T(4,128)} %param.7), kind=kLoop, calls=%fused_computation.79 | loop fusion | bytes 8388608 | tf_op jit(solution)/shard_map/slice | solution.py:284
  31.8 1.1 fusion.3
  32.8 2.5 convolution_add_fusion.3
  35.3 0.0 reduce-scatter.5.cloned.1.call-update
  35.4 0.0 reduce-scatter.7.cloned.1.call-start
  35.4 1.1 fusion.2
  36.5 2.5 convolution_add_fusion.2
  39.0 0.0 reduce-scatter.7.cloned.1.call-update
  39.0 0.0 reduce-scatter.9.cloned.1.call-start
  39.1 1.1 fusion.1
  40.1 2.5 convolution_add_fusion.1
  42.7 0.0 reduce-scatter.9.cloned.1.call-update
  42.7 0.2 reduce-scatter.11.cloned.1.call-start
  42.9 1.1 fusion
  44.0 2.5 convolution_add_fusion
  46.5 0.0 reduce-scatter.11.cloned.1.call-update
  46.6 2.2 slice_bitcast_fusion
  48.7 21.0 %reduce-scatter.5.cloned.1.call-done = f32[128,512]{0,1:T(8,128)} async-done(((f32[1024,512]{0,1:T(8,128)}), f32[128,512]{0,1:T(8,128)}) %reduce-scatter.5.cloned.1.call-update) | async-done | bytes 262160 | tf_op jit(solution)/shard_map/reduce_scatter | solution.py:286
  69.7 0.0 copy-start
  69.7 0.9 copy-done
  70.7 13.3 %first_step.1.refs_0_ = f32[512,128]{1,0:T(8,128)S(1)} custom-call(f32[512,128]{1,0:T(8,128)S(1)} %bitcast.61, f32[4,512,2048]{2,1,0:T(8,128)} %refs_2_.5), custom_call_target="tpu_custom_call" | custom-call | flops 1000000000 | bytes 60000000 | tf_op jit(solution)/shard_map/first_step/pallas_call | solution.py:83
  83.9 22.5 %reduce-scatter.7.cloned.1.call-done = f32[128,512]{0,1:T(8,128)} async-done(((f32[1024,512]{0,1:T(8,128)}), f32[128,512]{0,1:T(8,128)}) %reduce-scatter.7.cloned.1.call-update) | async-done | bytes 262160 | tf_op jit(solution)/shard_map/reduce_scatter | solution.py:286
  106.5 0.9 copy-done.2
  107.4 71.2 %block_step_1.1 = (f32[512,128]{1,0:T(8,128)S(1)}, f32[256,1024]{1,0:T(8,128)S(1)}, f32[256,1024]{1,0:T(8,128)S(1)}) custom-call(f32[512,128]{1,0:T(8,128)S(1)} %first_step.1.refs_0_, f32[512,128]{1,0:T(8,128)S(1)} %bitcast.63, f32[4,512,2048]{2,1,0:T(8,128)} %refs_2_.5, f32[256,512]{1,0:T(8,128)S(1)} %get-tuple-element.30.refs_3_, ...), custom_call_target="tpu_custom_call" | custom-call | flops 1000000000 | bytes 200000000 | tf_op jit(solution)/shard_map/block_step_1/pallas_call | solution.py:245
  178.6 0.0 copy-start.7
  178.6 0.7 copy-done.7
  179.3 0.0 copy-start.10
  179.3 1.0 copy-done.10
  180.2 0.0 copy-start.12
  180.2 1.0 copy-done.12
  181.2 0.0 reduce-scatter.9.cloned.1.call-done
  181.2 1.0 copy-done.4
  182.2 1.0 copy-done.8
  183.1 1.2 copy-done.11
  184.4 1.2 copy-done.13
  185.6 65.4 %block_step_2.1 = (f32[512,128]{1,0:T(8,128)S(1)}, f32[256,1024]{1,0:T(8,128)S(1)}) custom-call(f32[512,128]{1,0:T(8,128)S(1)} %copy-done.8, f32[512,128]{1,0:T(8,128)S(1)} %bitcast.65, f32[4,512,2048]{2,1,0:T(8,128)} %refs_2_.5, f32[256,512]{1,0:T(8,128)S(1)} %get-tuple-element.27.refs_3_, f32[256,512]{1,0:T(8,128)S(1)} %get-tuple-element.31.refs_4_, ...), custom_call_target="tpu_custom_call" | custom-call | flops 1000000000 | bytes 200000000 | tf_op jit(solution)/shard_map/block_step_2/pallas_call | solution.py:245
  251.0 0.0 reduce-scatter.11.cloned.1.call-done
  251.0 0.0 copy-start.6
  251.0 0.9 copy-done.6
  252.0 62.3 %block_step_3.1 = f32[512,128]{1,0:T(8,128)S(1)} custom-call(f32[512,128]{1,0:T(8,128)S(1)} %get-tuple-element.15.refs_0_, f32[512,128]{1,0:T(8,128)S(1)} %bitcast.67, f32[4,512,2048]{2,1,0:T(8,128)} %refs_2_.5, f32[256,512]{1,0:T(8,128)S(1)} %get-tuple-element.26.refs_3_, f32[256,1024]{1,0:T(8,128)S(1)} %get-tuple-element.16.refs_4_), custom_call_target="tpu_custom_call" | custom-call | flops 1000000000 | bytes 200000000 | tf_op jit(solution)/shard_map/block_step_3/pallas_call | solution.py:245
  314.3 0.0 copy-done.1
  314.3 0.0 copy-done.3
  314.3 0.0 copy-done.5
  314.3 0.0 copy-done.9
  314.3 1.5 pad_maximum_fusion
  (11 shorter events, 0.0 us)
Async XLA Ops:
  7.2 62.6 %reduce-scatter.5.cloned.1.call-start = ((), (), s32[]{:S(2)}) async-start(), calls=%async_computation.4 | async-start | bytes 2359296 | tf_op jit(solution)/shard_map/reduce_scatter | solution.py:286
  35.4 71.1 %reduce-scatter.7.cloned.1.call-start = ((), (), s32[]{:S(2)}) async-start(), calls=%async_computation.5 | async-start | bytes 2359296 | tf_op jit(solution)/shard_map/reduce_scatter | solution.py:286
  39.0 142.2 %reduce-scatter.9.cloned.1.call-start = ((), (), s32[]{:S(2)}) async-start(), calls=%async_computation.6 | async-start | bytes 2359296 | tf_op jit(solution)/shard_map/reduce_scatter | solution.py:286
  42.7 208.3 %reduce-scatter.11.cloned.1.call-start = ((), (), s32[]{:S(2)}) async-start(), calls=%async_computation.7 | async-start | bytes 2359296 | tf_op jit(solution)/shard_map/reduce_scatter | solution.py:286
  69.7 0.9 copy-start
  106.5 0.9 copy-start.2
  178.6 0.7 copy-start.7
  179.3 1.0 copy-start.10
  180.2 1.0 copy-start.12
  181.2 1.0 copy-start.4
  182.2 1.0 copy-start.8
  183.1 1.2 copy-start.11
  184.4 1.2 copy-start.13
  251.0 1.0 copy-start.6
  252.0 62.3 %copy-start.1 = (f32[128,512]{0,1:T(8,128)S(1)}, f32[128,512]{0,1:T(8,128)}, u32[]{:S(2)}) copy-start(f32[128,512]{0,1:T(8,128)} %reduce-scatter.5.cloned.1.call-done) | copy-start | bytes 786436
  252.0 62.3 %copy-start.3 = (f32[128,512]{0,1:T(8,128)S(1)}, f32[128,512]{0,1:T(8,128)}, u32[]{:S(2)}) copy-start(f32[128,512]{0,1:T(8,128)} %reduce-scatter.7.cloned.1.call-done) | copy-start | bytes 786436
  252.0 62.3 %copy-start.5 = (f32[128,512]{0,1:T(8,128)S(1)}, f32[128,512]{0,1:T(8,128)}, u32[]{:S(2)}) copy-start(f32[128,512]{0,1:T(8,128)} %reduce-scatter.9.cloned.1.call-done) | copy-start | bytes 786436
  252.0 62.4 %copy-start.9 = (f32[512,128]{1,0:T(8,128)S(1)}, f32[512,128]{1,0:T(8,128)}, u32[]{:S(2)}) copy-start(f32[512,128]{1,0:T(8,128)} %copy-done.7) | copy-start | bytes 786436
Sparse Core Ops, SparseCore 0:
  35.5 34.1 reduce-scatter.4
  72.0 34.3 reduce-scatter.6
  108.8 45.9 reduce-scatter.8
  156.9 43.0 reduce-scatter.10

commit v2 on v1

--- a/solution.py
+++ b/solution.py
@@ -279,9 +279,10 @@
         + (both[1][:, None] == owned[None, :]).astype(jnp.float32)
     )
     picks = picks.astype(jnp.bfloat16)
+    flat_rows = relatives.reshape(old_dev, blocks * block_cols)
     relationship = []
     for target in range(blocks):
-        high, low = split_exact(relatives[:, target, :])
+        high, low = split_exact(flat_rows[:, target * block_cols : (target + 1) * block_cols])
         shares = mxu(picks, high) + mxu(picks, low)
         relationship.append(lax.psum_scatter(shares, "row", scatter_dimension=0, tiled=True).T)
     solved = [first_step(cols, relationship[0], inverses)]

time: 323 us -> 318 us (0.985)
  matrix products: 14.3 us -> 21.8 us
  waiting for transfers between devices: 43.6 us -> 36.4 us
  local copies, waits for them, and re-layouts: 22.4 us -> 17.1 us
    slice x1 -> x0, local copies, waits for them, and re-layouts: 10.4 us -> none  [per_device(): high, low = split_exact(relatives[:, target, :])]
    dot_general x8, matrix products: 14.3 us -> 21.8 us  [mxu(): return jnp.dot(left, right, preferred_element_type=jnp.float32)]
    reduce_scatter x4, waiting for transfers between devices: 43.5 us -> 36.4 us  [per_device(): lax.psum_scatter(shares, 'row', scatter_dimension=0, tiled=True)]
    unnamed x28 -> x31, local copies, waits for them, and re-layouts: 9.86 us -> 14.9 us
  transfers between devices with their start and end apart: 4 -> 4, of which waited for: 2 -> 2; matrix products, arithmetic and copies ran while one was open for 4% -> 6% of each run, Pallas kernels for 46% -> 47%
where the time goes in v2:
time: 318 us; the launch traced here: 317 us
  Pallas kernels  212 us (67%)
  waiting for transfers between devices  36.4 us (11%)
  matrix products  21.8 us (7%)
  local copies, waits for them, and re-layouts  17.1 us (5%)
  between operations  13.9 us (4%)
  blocking collectives  13.5 us (4%)
    pallas_call x3, Pallas kernels, block_step(): pl.pallas_call(functools.partial(step_kernel, target, rows, cols, later,...  198 us
    reduce_scatter x4, waiting for transfers between devices, per_device(): lax.psum_scatter(shares, 'row', scatter_dimension=0, tiled=True)  36.4 us
    dot_general x8, matrix products, mxu(): return jnp.dot(left, right, preferred_element_type=jnp.float32)  21.8 us
    unnamed x31, local copies, waits for them, and re-layouts  14.9 us
    all_gather x1, blocking collectives, per_device(): lax.all_gather(jnp.stack([sire_index, dam_index]), 'row', axis=1, tiled=T...  13.5 us
    pallas_call x1, Pallas kernels, first_step(): pl.pallas_call(functools.partial(first_kernel, 0, cols), out_shape=jax.Sh...  13.2 us
  transfers between devices with their start and end apart: 4, of which 2 were waited for; matrix products, arithmetic and copies ran while one was open for 6% of the time, Pallas kernels for 47%

profile of v2, /device:TPU:0, one launch (start us, length us, event | category | flops | bytes accessed | tf_op | source)
XLA Modules:
  0.0 316.9 jit_solution(11899799016058162552)
XLA Ops:
  7.2 0.0 reduce-scatter.5.cloned.1.call-start
  7.2 0.7 pad_add_fusion
  7.9 13.5 %all_gather.3 = s32[2,1024]{1,0:T(2,128)S(1)} all-gather(s32[2,128]{1,0:T(2,128)S(1)} %pad_add_fusion), channel_id=1, replica_groups=mesh['row'=8,'col'=4] {'row'}, dimensions={1}, use_global_device_ids=true | all-gather | bytes 9216 | tf_op jit(solution)/shard_map/all_gather | solution.py:275
  21.4 4.1 %copy.23 = f32[64,8,4,512]{3,1,2,0:T(8,128)S(1)} copy(f32[64,8,4,512]{3,2,1,0:T(4,128)} %bitcast.42) | data formatting | bytes 8388608
  25.5 0.0 copy-start.14
  25.5 1.1 fusion.3
  26.6 0.9 copy-done.14
  27.5 2.5 convolution_add_fusion.3
  30.0 0.0 reduce-scatter.5.cloned.1.call-update
  30.0 0.0 reduce-scatter.7.cloned.1.call-start
  30.0 2.3 fusion.2
  32.3 3.8 %convolution_add_fusion.2 = f32[1024,512]{0,1:T(8,128)} fusion(f32[1024,512]{0,1:T(8,128)S(1)} %fusion.2, s32[512]{0:T(512)S(1)} %iota_add_fusion, s32[1024]{0:T(1024)S(1)} %bitcast.62, s32[1024]{0:T(1024)S(1)} %bitcast.54, f32[512,2048]{1,0:T(8,128)} %bitcast.46), kind=kOutput, calls=%fused_computation.3 | convolution fusion | flops 542113792 | bytes 5253120 | tf_op jit(solution)/shard_map/dot_general | solution.py:24
  36.1 0.0 reduce-scatter.7.cloned.1.call-update
  36.2 0.0 reduce-scatter.9.cloned.1.call-start
  36.2 2.3 fusion.1
  38.5 3.8 %convolution_add_fusion.1 = f32[1024,512]{0,1:T(8,128)} fusion(f32[1024,512]{0,1:T(8,128)S(1)} %fusion.1, s32[512]{0:T(512)S(1)} %iota_add_fusion, s32[1024]{0:T(1024)S(1)} %bitcast.64, s32[1024]{0:T(1024)S(1)} %bitcast.56, f32[512,2048]{1,0:T(8,128)} %bitcast.48), kind=kOutput, calls=%fused_computation.2 | convolution fusion | flops 542113792 | bytes 5253120 | tf_op jit(solution)/shard_map/dot_general | solution.py:24
  42.3 0.0 reduce-scatter.9.cloned.1.call-update
  42.3 0.2 reduce-scatter.11.cloned.1.call-start
  42.5 2.3 fusion
  44.8 3.8 %convolution_add_fusion = f32[1024,512]{0,1:T(8,128)} fusion(f32[1024,512]{0,1:T(8,128)S(1)} %fusion, s32[512]{0:T(512)S(1)} %iota_add_fusion, s32[1024]{0:T(1024)S(1)} %bitcast.66, s32[1024]{0:T(1024)S(1)} %bitcast.58, f32[512,2048]{1,0:T(8,128)} %bitcast.50), kind=kOutput, calls=%fused_computation.1 | convolution fusion | flops 542113792 | bytes 5253120 | tf_op jit(solution)/shard_map/dot_general | solution.py:24
  48.6 0.0 reduce-scatter.11.cloned.1.call-update
  48.6 2.2 slice_bitcast_fusion
  50.8 13.6 %reduce-scatter.5.cloned.1.call-done = f32[128,512]{0,1:T(8,128)} async-done(((f32[1024,512]{0,1:T(8,128)}), f32[128,512]{0,1:T(8,128)}) %reduce-scatter.5.cloned.1.call-update) | async-done | bytes 262160 | tf_op jit(solution)/shard_map/reduce_scatter | solution.py:287
  64.4 0.0 copy-start
  64.4 0.9 copy-done
  65.3 13.2 %first_step.1.refs_0_ = f32[512,128]{1,0:T(8,128)S(1)} custom-call(f32[512,128]{1,0:T(8,128)S(1)} %bitcast.31, f32[4,512,2048]{2,1,0:T(8,128)} %refs_2_.5), custom_call_target="tpu_custom_call" | custom-call | flops 1000000000 | bytes 60000000 | tf_op jit(solution)/shard_map/first_step/pallas_call | solution.py:83
  78.6 22.8 %reduce-scatter.7.cloned.1.call-done = f32[128,512]{0,1:T(8,128)} async-done(((f32[1024,512]{0,1:T(8,128)}), f32[128,512]{0,1:T(8,128)}) %reduce-scatter.7.cloned.1.call-update) | async-done | bytes 262160 | tf_op jit(solution)/shard_map/reduce_scatter | solution.py:287
  101.4 0.0 copy-start.2
  101.4 0.9 copy-done.2
  102.3 71.1 %block_step_1.1 = (f32[512,128]{1,0:T(8,128)S(1)}, f32[256,1024]{1,0:T(8,128)S(1)}, f32[256,1024]{1,0:T(8,128)S(1)}) custom-call(f32[512,128]{1,0:T(8,128)S(1)} %first_step.1.refs_0_, f32[512,128]{1,0:T(8,128)S(1)} %bitcast.33, f32[4,512,2048]{2,1,0:T(8,128)} %refs_2_.5, f32[256,512]{1,0:T(8,128)S(1)} %get-tuple-element.26.refs_3_, ...), custom_call_target="tpu_custom_call" | custom-call | flops 1000000000 | bytes 200000000 | tf_op jit(solution)/shard_map/block_step_1/pallas_call | solution.py:245
  173.4 0.0 copy-start.7
  173.4 0.7 copy-done.7
  174.1 1.0 copy-done.10
  175.1 1.0 copy-done.12
  176.1 1.0 copy-done.4
  177.0 1.0 copy-done.8
  178.0 1.2 copy-done.11
  179.2 1.2 copy-done.13
  180.5 64.9 %block_step_2.1 = (f32[512,128]{1,0:T(8,128)S(1)}, f32[256,1024]{1,0:T(8,128)S(1)}) custom-call(f32[512,128]{1,0:T(8,128)S(1)} %copy-done.8, f32[512,128]{1,0:T(8,128)S(1)} %bitcast.35, f32[4,512,2048]{2,1,0:T(8,128)} %refs_2_.5, f32[256,512]{1,0:T(8,128)S(1)} %get-tuple-element.23.refs_3_, f32[256,512]{1,0:T(8,128)S(1)} %get-tuple-element.27.refs_4_, ...), custom_call_target="tpu_custom_call" | custom-call | flops 1000000000 | bytes 200000000 | tf_op jit(solution)/shard_map/block_step_2/pallas_call | solution.py:245
  245.4 0.0 reduce-scatter.11.cloned.1.call-done
  245.4 0.0 copy-start.6
  245.4 0.9 copy-done.6
  246.4 62.4 %block_step_3.1 = f32[512,128]{1,0:T(8,128)S(1)} custom-call(f32[512,128]{1,0:T(8,128)S(1)} %get-tuple-element.15.refs_0_, f32[512,128]{1,0:T(8,128)S(1)} %bitcast.37, f32[4,512,2048]{2,1,0:T(8,128)} %refs_2_.5, f32[256,512]{1,0:T(8,128)S(1)} %get-tuple-element.22.refs_3_, f32[256,1024]{1,0:T(8,128)S(1)} %get-tuple-element.16.refs_4_), custom_call_target="tpu_custom_call" | custom-call | flops 1000000000 | bytes 200000000 | tf_op jit(solution)/shard_map/block_step_3/pallas_call | solution.py:245
  308.8 0.0 copy-done.1
  308.8 0.0 copy-done.3
  308.8 0.0 copy-done.5
  308.9 0.0 copy-done.9
  308.9 1.5 pad_maximum_fusion
  (13 shorter events, 0.0 us)
Async XLA Ops:
  7.2 57.2 %reduce-scatter.5.cloned.1.call-start = ((), (), s32[]{:S(2)}) async-start(), calls=%async_computation.4 | async-start | bytes 2359296 | tf_op jit(solution)/shard_map/reduce_scatter | solution.py:287
  25.5 2.0 copy-start.14
  30.0 71.4 %reduce-scatter.7.cloned.1.call-start = ((), (), s32[]{:S(2)}) async-start(), calls=%async_computation.5 | async-start | bytes 2359296 | tf_op jit(solution)/shard_map/reduce_scatter | solution.py:287
  36.2 139.9 %reduce-scatter.9.cloned.1.call-start = ((), (), s32[]{:S(2)}) async-start(), calls=%async_computation.6 | async-start | bytes 2359296 | tf_op jit(solution)/shard_map/reduce_scatter | solution.py:287
  42.3 203.1 %reduce-scatter.11.cloned.1.call-start = ((), (), s32[]{:S(2)}) async-start(), calls=%async_computation.7 | async-start | bytes 2359296 | tf_op jit(solution)/shard_map/reduce_scatter | solution.py:287
  64.4 0.9 copy-start
  101.4 0.9 copy-start.2
  173.4 0.7 copy-start.7
  174.1 1.0 copy-start.10
  175.1 1.0 copy-start.12
  176.1 1.0 copy-start.4
  177.0 1.0 copy-start.8
  178.0 1.2 copy-start.11
  179.2 1.2 copy-start.13
  245.4 1.0 copy-start.6
  246.4 62.5 %copy-start.1 = (f32[128,512]{0,1:T(8,128)S(1)}, f32[128,512]{0,1:T(8,128)}, u32[]{:S(2)}) copy-start(f32[128,512]{0,1:T(8,128)} %reduce-scatter.5.cloned.1.call-done) | copy-start | bytes 786436
  246.4 62.5 %copy-start.3 = (f32[128,512]{0,1:T(8,128)S(1)}, f32[128,512]{0,1:T(8,128)}, u32[]{:S(2)}) copy-start(f32[128,512]{0,1:T(8,128)} %reduce-scatter.7.cloned.1.call-done) | copy-start | bytes 786436
  246.4 62.5 %copy-start.5 = (f32[128,512]{0,1:T(8,128)S(1)}, f32[128,512]{0,1:T(8,128)}, u32[]{:S(2)}) copy-start(f32[128,512]{0,1:T(8,128)} %reduce-scatter.9.cloned.1.call-done) | copy-start | bytes 786436
  246.4 62.5 %copy-start.9 = (f32[512,128]{1,0:T(8,128)S(1)}, f32[512,128]{1,0:T(8,128)}, u32[]{:S(2)}) copy-start(f32[512,128]{1,0:T(8,128)} %copy-done.7) | copy-start | bytes 786436
Sparse Core Ops, SparseCore 0:
  30.1 34.2 reduce-scatter.4
  66.7 34.6 reduce-scatter.6
  103.7 46.3 reduce-scatter.8
  152.2 42.3 reduce-scatter.10
